TPU v7x, 32 devices: a whole 2x2x4 slice. The times are simulated.
32 devices in a mesh: seq: 8 (over z, core), batch: 4 (over y, x).
Axes of the slice: x: 2, y: 2, z: 4, core: 2. Of those that a mesh axis runs over, the one named last changes fastest.
Arguments:
- inputs: bfloat16 [4, 64, 8192], P('batch'), may hold values from -6 to 6
- w_query: bfloat16 [8192, 8192], P('batch', 'seq'), may hold values from -0.0625 to 0.0625
- cache_keys: bfloat16 [4, 4096, 1024], P('batch', 'seq'), may hold values from -120 to 120
- cache_values: bfloat16 [4, 4096, 1024], P('batch', 'seq'), may hold values from -6 to 6
- lengths: int32 [4], P('batch'), may hold values from 1 to 4096, as said below
- positions: int32 [4, 64], P('batch'), may hold values from 0 to 4095, as said below
Outputs:
- attended: bfloat16 [4, 64, 8192], P('batch', None, 'seq')
Inputs may be any that keep to these rules, and one draw needn't show every extreme that they name: `lengths`: every sample has at least one valid position; some sample has all 4096 valid. `positions`: some query sits at position 0 and some at 4095.
All inputs are finite; a program needn't handle non-finite values.
Results may differ from a plain program's by a relative error of at most 0.015.
The roundings to bfloat16 on the way count: a program that leaves them out, or rounds other values in their place, can miss the bound.
Values may be sent and summed in bfloat16 or wider, within the bound.
No kernel may reach another device: no remote copies, remote signals or barrier semaphores. Data moves between devices by JAX's collectives and lax.ppermute only.
A program may use at most 64 MiB of HBM per device.

v0:
```python
import functools

import jax
import jax.numpy as jnp
from jax import lax
from jax.experimental import pallas as pl
from jax.experimental.pallas import tpu as pltpu
from jax.sharding import PartitionSpec as P


H = 64
KVH = 8
HD = 128


ANY = pl.BlockSpec(memory_space=pl.ANY)
HBM = pl.BlockSpec(memory_space=pltpu.HBM)
VMEM = pl.BlockSpec(memory_space=pltpu.VMEM)
SMEM = pl.BlockSpec(memory_space=pltpu.SMEM)
SMALL = pltpu.CompilerParams(vmem_limit_bytes=24 << 20)
LOG2E = 1.4426950408889634
NONE_VISIBLE = -1e30


def peers(count, step):
    if count & (count - 1) == 0:
        return [(j, j ^ step) for j in range(count)]
    return [(j, (j + step) % count) for j in range(count)]


def target(me, count, step):
    return me ^ step if count & (count - 1) == 0 else lax.rem(me + step, count)


def source(me, count, step):
    return me ^ step if count & (count - 1) == 0 else lax.rem(me + count - step, count)


def seq_order(count):
    half = count // 2
    far = [*range(half + 2, count, 2), *range(half + 1, count, 2)]
    return [half, *range(2, half), *far, 1]


def pack_cache(key_rows, value_rows, seq_count, steps):
    keys_here, width = key_rows.shape
    share = width // seq_count

    def kernel(keys, values, *rest):
        outs, sem = rest[:-1], rest[-1]
        me = lax.axis_index("seq")
        copies = []
        for n, step in enumerate(steps):
            columns = pl.ds(pl.multiple_of(target(me, seq_count, step) * share, share), share)
            for part, rows in enumerate((keys, values)):
                copy = pltpu.make_async_copy(rows.at[:, columns], outs[n].at[part], sem.at[n, part])
                copy.start()
                copies.append(copy)
        for copy in copies:
            copy.wait()

    return pl.pallas_call(
        kernel,
        out_shape=[jax.ShapeDtypeStruct((2, keys_here, share), key_rows.dtype)] * len(steps),
        in_specs=[HBM, HBM],
        out_specs=[VMEM] * len(steps),
        scratch_shapes=[pltpu.SemaphoreType.DMA((len(steps), 2))],
        cost_estimate=pl.CostEstimate(
            flops=0, transcendentals=0, bytes_accessed=len(steps) * 8 * keys_here * share
        ),
        compiler_params=SMALL,
        name="pack_cache",
    )(key_rows, value_rows)


def pack_features(tokens, batch_count):
    rows, width = tokens.shape
    share = width // batch_count

    def kernel(tokens_ref, *rest):
        outs, sem = rest[:-1], rest[-1]
        me = lax.axis_index("batch")
        copies = []
        for step in range(batch_count):
            columns = pl.ds(pl.multiple_of(target(me, batch_count, step) * share, share), share)
            copy = pltpu.make_async_copy(tokens_ref.at[:, columns], outs[step], sem.at[step])
            copy.start()
            copies.append(copy)
        for copy in copies:
            copy.wait()

    return pl.pallas_call(
        kernel,
        out_shape=[jax.ShapeDtypeStruct((rows, share), tokens.dtype)] * batch_count,
        in_specs=[HBM],
        out_specs=[VMEM] * batch_count,
        scratch_shapes=[pltpu.SemaphoreType.DMA((batch_count,))],
        cost_estimate=pl.CostEstimate(flops=0, transcendentals=0, bytes_accessed=4 * rows * width),
        compiler_params=SMALL,
        name="pack_features",
    )(tokens)


def project(blocks, weight):
    count = len(blocks)
    rows, depth = blocks[0].shape
    columns = weight.shape[1]
    tile = min(256, columns)

    def kernel(*refs):
        ins, w_ref, outs, stacked = refs[:count], refs[count], refs[count + 1 : -1], refs[-1]

        @pl.when(pl.program_id(0) == 0)
        def _():
            for n in range(count):
                stacked[pl.ds(n * rows, rows), :] = ins[n][...]

        product = jnp.dot(stacked[...], w_ref[...], preferred_element_type=jnp.float32)
        for n in range(count):
            outs[n][...] = product[n * rows : (n + 1) * rows]

    return pl.pallas_call(
        kernel,
        grid=(columns // tile,),
        out_shape=[jax.ShapeDtypeStruct((rows, columns), jnp.float32)] * count,
        in_specs=[pl.BlockSpec((rows, depth), lambda j: (0, 0))] * count
        + [pl.BlockSpec((depth, tile), lambda j: (0, j))],
        out_specs=[pl.BlockSpec((rows, tile), lambda j: (0, j))] * count,
        scratch_shapes=[pltpu.VMEM((count * rows, depth), blocks[0].dtype)],
        cost_estimate=pl.CostEstimate(
            flops=2 * count * rows * depth * columns,
            transcendentals=0,
            bytes_accessed=2 * depth * columns + 6 * count * rows * depth,
        ),
        compiler_params=SMALL,
        name="project",
    )(*blocks, weight)


def attend(query, chunks, steps, state, positions, lengths, seq_count, last):
    first = state is None
    tokens = positions.shape[1]
    group = H // KVH
    columns = group * tokens
    n_query = len(query)
    n_chunks = len(chunks)
    keys_here = chunks[0].shape[-2]
    moved = [*query, *chunks]
    inputs = [lengths, positions, *moved] + ([] if first else list(state))
    state_shape = [
        jax.ShapeDtypeStruct((1, columns), jnp.float32),
        jax.ShapeDtypeStruct((1, columns), jnp.float32),
        jax.ShapeDtypeStruct((HD, columns), jnp.float32),
    ]
    if last:
        out_shape = [jax.ShapeDtypeStruct((tokens, group * HD), jnp.bfloat16)]
    else:
        out_shape = state_shape
        if first:
            out_shape = out_shape + [jax.ShapeDtypeStruct((columns, HD), jnp.bfloat16)]

    def kernel(*refs):
        lengths_ref, positions_ref = refs[:2]
        moved_refs = refs[2 : 2 + len(moved)]
        state_refs = refs[2 + len(moved) : len(inputs)]
        outs = refs[len(inputs) : len(inputs) + len(out_shape)]
        held = refs[len(inputs) + len(out_shape) : -1]
        sem = refs[-1]
        copies = [
            pltpu.make_async_copy(src, dst, sem.at[n]) for n, (src, dst) in enumerate(zip(moved_refs, held))
        ]
        for copy in copies:
            copy.start()
        me = lax.axis_index("seq")
        limit = jnp.minimum(positions_ref[...], lengths_ref[0] - 1)
        limit = jnp.concatenate([limit] * group, axis=1)
        rows = lax.broadcasted_iota(jnp.int32, (keys_here, columns), 0)
        for copy in copies[:n_query]:
            copy.wait()
        if first:
            total = held[0][...]
            for ref in held[1:n_query]:
                total = total + ref[...]
            rounded = total.astype(jnp.bfloat16)
            q = jnp.concatenate([rounded[:, h * HD : (h + 1) * HD] for h in range(group)], axis=0)
            if not last:
                outs[3][...] = q
            top = denom = numer = None
        else:
            q = held[0][...]
            top, denom, numer = (ref[...] for ref in state_refs)
        for n, step in enumerate(steps):
            start = source(me, seq_count, step) * keys_here
            copies[n_query + n].wait()
            ref = held[n_query + n]
            score = lax.dot_general(
                ref[0], q, (((1,), (1,)), ((), ())), preferred_element_type=jnp.float32
            )
            score = jnp.where(rows <= limit - start, score, NONE_VISIBLE)
            block_max = jnp.max(score, axis=0, keepdims=True)
            expo = jnp.exp2((score - block_max) * (HD**-0.5 * LOG2E))
            block_total = jnp.sum(expo, axis=0, keepdims=True)
            block_sum = lax.dot_general(
                ref[1],
                expo.astype(jnp.bfloat16),
                (((0,), (0,)), ((), ())),
                preferred_element_type=jnp.float32,
            )
            block_sum = block_sum.astype(jnp.bfloat16).astype(jnp.float32)
            if top is None:
                top, denom, numer = block_max, block_total, block_sum
                continue
            new_top = jnp.maximum(top, block_max)
            keep = jnp.exp2((top - new_top) * (HD**-0.5 * LOG2E))
            weight = jnp.exp2((block_max - new_top) * (HD**-0.5 * LOG2E))
            denom = denom * keep + block_total * weight
            numer = numer * keep + block_sum * weight
            top = new_top
        if last:
            result = numer / denom
            for h in range(group):
                part = result[:, h * tokens : (h + 1) * tokens]
                outs[0][:, h * HD : (h + 1) * HD] = jnp.transpose(part).astype(jnp.bfloat16)
        else:
            outs[0][...] = top
            outs[1][...] = denom
            outs[2][...] = numer

    return pl.pallas_call(
        kernel,
        out_shape=out_shape,
        in_specs=[SMEM, VMEM] + [ANY] * len(moved) + [VMEM] * (len(inputs) - 2 - len(moved)),
        out_specs=[VMEM] * len(out_shape),
        scratch_shapes=[pltpu.VMEM(x.shape, x.dtype) for x in moved]
        + [pltpu.SemaphoreType.DMA((len(moved),))],
        cost_estimate=pl.CostEstimate(
            flops=4 * n_chunks * keys_here * columns * HD,
            transcendentals=n_chunks * keys_here * columns,
            bytes_accessed=n_chunks * 4 * keys_here * HD,
        ),
        compiler_params=SMALL,
        name="attend",
    )(*inputs)


def own_heads(inputs, w_query, cache_keys, cache_values, lengths, positions):
    seq_count = lax.axis_size("seq")
    batch_count = lax.axis_size("batch")
    order = seq_order(seq_count)
    key_rows, value_rows, tokens = cache_keys[0], cache_values[0], inputs[0]
    packed = pack_cache(key_rows, value_rows, seq_count, order[:3])
    blocks = list(pack_features(tokens, batch_count))
    packed = [*packed, *pack_cache(key_rows, value_rows, seq_count, [*order[3:], 0])]
    moved = {0: packed[-1]}
    for step, block in zip(order, packed):
        moved[step] = lax.ppermute(block, "seq", peers(seq_count, step))
    for step in range(1, batch_count):
        blocks[step] = lax.ppermute(blocks[step], "batch", peers(batch_count, step))
    partials = project(blocks, w_query)
    back = [partials[0]]
    for step in range(1, batch_count):
        back.append(lax.ppermute(partials[step], "batch", [(b, a) for a, b in peers(batch_count, step)]))
    attend_ = functools.partial(attend, positions=positions, lengths=lengths, seq_count=seq_count)
    half = seq_count // 2
    early, middle, late = [*range(half), order[0]], order[half - 1 : -2], order[-2:-1]
    *state, query = attend_(back, [moved[s] for s in early], early, None, last=False)
    state = attend_([query], [moved[s] for s in middle], middle, state, last=False)
    (out,) = attend_([query], [moved[s] for s in late], late, state, last=True)
    return out[None]


def split_positions(inputs, w_query, cache_keys, cache_values, lengths, positions):
    seq_count = lax.axis_size("seq")
    heads_here = H // seq_count
    group = H // KVH
    keys_here = cache_keys.shape[1]
    tokens = inputs[0]
    query_rows = tokens.shape[0]
    features = lax.all_to_all(inputs, "batch", split_axis=2, concat_axis=0, tiled=True)
    query = lax.psum_scatter(
        jnp.einsum("sqd,dc->sqc", features, w_query, preferred_element_type=jnp.float32),
        "batch",
        scatter_dimension=0,
        tiled=True,
    )[0]
    query = query.astype(jnp.bfloat16)
    all_query = lax.all_gather(query, "seq", axis=1, tiled=True)
    query_heads = all_query.reshape(query_rows, KVH, group, HD)
    key_pos = lax.axis_index("seq") * keys_here + jnp.arange(keys_here, dtype=jnp.int32)
    visible = (key_pos[None, :] <= positions[0][:, None]) & (key_pos[None, :] < lengths[0])
    key_rows = cache_keys[0]
    value_rows = cache_values[0]

    def one_head(kv_head):
        key_block = lax.dynamic_slice_in_dim(key_rows, kv_head * HD, HD, 1)
        value_block = lax.dynamic_slice_in_dim(value_rows, kv_head * HD, HD, 1)
        query_group = lax.dynamic_index_in_dim(query_heads, kv_head, 1, keepdims=False)
        score = jnp.einsum(
            "qrd,kd->rqk", query_group, key_block, preferred_element_type=jnp.float32
        ) * HD ** (-0.5)
        block_max = jnp.max(jnp.where(visible[None], score, -1e30), axis=-1)
        expo = jnp.where(visible[None], jnp.exp(score - block_max[..., None]), 0.0)
        block_total = jnp.sum(expo, axis=-1)
        prob = expo.astype(jnp.bfloat16)
        block_sum = jnp.einsum(
            "rqk,kd->rqd", prob, value_block, preferred_element_type=jnp.float32
        ).astype(jnp.bfloat16)
        return (block_sum, block_max, block_total)

    sums, maxima, totals = lax.map(one_head, jnp.arange(KVH, dtype=jnp.int32))
    sums = sums.reshape(1, H, query_rows, HD)
    maxima = maxima.reshape(1, H, query_rows)
    totals = totals.reshape(1, H, query_rows)
    got_sums = lax.all_to_all(sums, "seq", split_axis=1, concat_axis=0, tiled=True)
    got_max, got_total = (
        lax.all_to_all(maxima, "seq", split_axis=1, concat_axis=0, tiled=True),
        lax.all_to_all(totals, "seq", split_axis=1, concat_axis=0, tiled=True),
    )
    top = jnp.max(got_max, axis=0)
    weight = jnp.exp(got_max - top[None])
    numer = jnp.sum(weight[..., None] * got_sums.astype(jnp.float32), axis=0)
    denom = jnp.sum(weight * got_total, axis=0)
    result = numer / denom[..., None]
    return (
        jnp.transpose(result, (1, 0, 2))
        .reshape(query_rows, heads_here * HD)[None]
        .astype(jnp.bfloat16)
    )


def solution(mesh):
    in_specs = (
        P("batch", None, None),
        P("batch", "seq"),
        P("batch", "seq", None),
        P("batch", "seq", None),
        P("batch"),
        P("batch", None),
    )
    out_specs = P("batch", None, "seq")
    split = functools.partial(
        jax.shard_map, mesh=mesh, in_specs=in_specs, out_specs=out_specs, check_vma=False
    )
    if mesh.shape["seq"] != KVH:
        return split(split_positions)
    return split(own_heads)
```

profile of v0, /device:TPU:1, one launch (start us, length us, event | category | flops | bytes accessed | tf_op | source)
XLA Modules:
  0.0 64.2 jit_solution(6787904247372210000)
XLA Ops:
  0.0 1.4 %copy-done.3 = bf16[1,64,8192]{2,1,0:T(8,128)(2,1)S(1)} copy-done((bf16[1,64,8192]{2,1,0:T(8,128)(2,1)S(1)}, bf16[1,64,8192]{2,1,0:T(8,128)(2,1)}, u32[]{:S(2)}) %copy-start.3) | copy-done | bytes 1048600
  1.4 0.1 pack_features.1
  1.5 2.1 %collective-permute-start = (bf16[64,2048]{1,0:T(8,128)(2,1)S(1)}, bf16[64,2048]{1,0:T(8,128)(2,1)S(1)}, u32[]{:S(2)}, u32[]{:S(2)}) collective-permute-start(bf16[64,2048]{1,0:T(8,128)(2,1)S(1)} %get-tuple-element.29), channel_id=1, source_target_pairs={{0,1},{1,0},{2,3},{3,2},{4,5},{5,4},{6,7},{7,6},{8,9},{9,8},{10,11... | collective-permute-start | bytes 786440 | tf_op jit(solution)/shard_map/ppermute | solution.py:258
  3.6 1.2 %collective-permute-start.1 = (bf16[64,2048]{1,0:T(8,128)(2,1)S(1)}, bf16[64,2048]{1,0:T(8,128)(2,1)S(1)}, u32[]{:S(2)}, u32[]{:S(2)}) collective-permute-start(bf16[64,2048]{1,0:T(8,128)(2,1)S(1)} %get-tuple-element.30), channel_id=1, source_target_pairs={{0,2},{1,3},{2,0},{3,1},{4,6},{5,7},{6,4},{7,5},{8,10},{9,11},{10,... | collective-permute-start | bytes 786440 | tf_op jit(solution)/shard_map/ppermute | solution.py:258
  4.8 0.0 collective-permute-start.2
  4.9 1.2 %copy-done.1 = bf16[1,512,1024]{2,1,0:T(8,128)(2,1)S(1)} copy-done((bf16[1,512,1024]{2,1,0:T(8,128)(2,1)S(1)}, bf16[1,512,1024]{2,1,0:T(8,128)(2,1)}, u32[]{:S(2)}) %copy-start.1) | copy-done | bytes 1048600
  6.1 1.2 %copy-done.2 = bf16[1,512,1024]{2,1,0:T(8,128)(2,1)S(1)} copy-done((bf16[1,512,1024]{2,1,0:T(8,128)(2,1)S(1)}, bf16[1,512,1024]{2,1,0:T(8,128)(2,1)}, u32[]{:S(2)}) %copy-start.2) | copy-done | bytes 1048600
  7.3 0.3 pack_cache.3
  7.6 0.0 copy-start.4
  7.6 1.5 %collective-permute-start.7 = (bf16[2,512,128]{2,1,0:T(8,128)(2,1)S(1)}, bf16[2,512,128]{2,1,0:T(8,128)(2,1)S(1)}, u32[]{:S(2)}, u32[]{:S(2)}) collective-permute-start(bf16[2,512,128]{2,1,0:T(8,128)(2,1)S(1)} %get-tuple-element.38), channel_id=1, source_target_pairs={{0,8},{4,12},{8,0},{12,4},{16,24},{20,28},{24,16},{28,20},{1,9},{5... | collective-permute-start | bytes 786440 | tf_op jit(solution)/shard_map/ppermute | solution.py:256
  9.1 1.5 %collective-permute-start.8 = (bf16[2,512,128]{2,1,0:T(8,128)(2,1)S(1)}, bf16[2,512,128]{2,1,0:T(8,128)(2,1)S(1)}, u32[]{:S(2)}, u32[]{:S(2)}) collective-permute-start(bf16[2,512,128]{2,1,0:T(8,128)(2,1)S(1)} %get-tuple-element.39), channel_id=1, source_target_pairs={{0,12},{4,8},{8,4},{12,0},{16,28},{20,24},{24,20},{28,16},{1,13},{... | collective-permute-start | bytes 786440 | tf_op jit(solution)/shard_map/ppermute | solution.py:256
  10.6 0.5 pack_cache.2
  11.1 0.0 collective-permute-done.refs_1_
  11.1 2.7 %collective-permute-start.9 = (bf16[2,512,128]{2,1,0:T(8,128)(2,1)S(1)}, bf16[2,512,128]{2,1,0:T(8,128)(2,1)S(1)}, u32[]{:S(2)}, u32[]{:S(2)}) collective-permute-start(bf16[2,512,128]{2,1,0:T(8,128)(2,1)S(1)} %get-tuple-element.40), channel_id=1, source_target_pairs={{0,16},{4,20},{8,24},{12,28},{16,0},{20,4},{24,8},{28,12},{1,17},{... | collective-permute-start | bytes 786440 | tf_op jit(solution)/shard_map/ppermute | solution.py:256
  13.9 4.1 %collective-permute-start.6 = (bf16[2,512,128]{2,1,0:T(8,128)(2,1)S(1)}, bf16[2,512,128]{2,1,0:T(8,128)(2,1)S(1)}, u32[]{:S(2)}, u32[]{:S(2)}) collective-permute-start(bf16[2,512,128]{2,1,0:T(8,128)(2,1)S(1)} %get-tuple-element.37), channel_id=1, source_target_pairs={{0,4},{4,0},{8,12},{12,8},{16,20},{20,16},{24,28},{28,24},{1,5},{5... | collective-permute-start | bytes 786440 | tf_op jit(solution)/shard_map/ppermute | solution.py:256
  17.9 0.0 collective-permute-done.2.refs_3_
  17.9 2.5 %project.1 = (f32[64,1024]{1,0:T(8,128)S(1)}, f32[64,1024]{1,0:T(8,128)S(1)}, f32[64,1024]{1,0:T(8,128)S(1)}, f32[64,1024]{1,0:T(8,128)S(1)}) custom-call(bf16[64,2048]{1,0:T(8,128)(2,1)S(1)} %get-tuple-element.28.refs_0_, bf16[64,2048]{1,0:T(8,128)(2,1)S(1)} %collective-permute-done.refs_1_, bf16[64,2048]{1,0:T(8,128)(2,1)S(1)} %collective-permute-done.1.refs_2_, ...), custom_call_target="tpu_custom_call" | custom-call | flops 1073741824 | bytes 7340032 | tf_op jit(solution)/shard_map/project/pallas_call | solution.py:122
  20.5 0.1 collective-permute-start.3
  20.5 0.0 collective-permute-done.7.refs_8_
  20.6 1.5 %collective-permute-start.4 = (f32[64,1024]{1,0:T(8,128)S(1)}, f32[64,1024]{1,0:T(8,128)S(1)}, u32[]{:S(2)}, u32[]{:S(2)}) collective-permute-start(f32[64,1024]{1,0:T(8,128)S(1)} %get-tuple-element.34), channel_id=1, source_target_pairs={{2,0},{3,1},{0,2},{1,3},{6,4},{7,5},{4,6},{5,7},{10,8},{11,9},{8,1... | collective-permute-start | bytes 786440 | tf_op jit(solution)/shard_map/ppermute | solution.py:262
  22.0 5.2 %collective-permute-done.8.refs_9_ = bf16[2,512,128]{2,1,0:T(8,128)(2,1)S(1)} collective-permute-done((bf16[2,512,128]{2,1,0:T(8,128)(2,1)S(1)}, bf16[2,512,128]{2,1,0:T(8,128)(2,1)S(1)}, u32[]{:S(2)}, u32[]{:S(2)}) %collective-permute-start.8) | collective-permute-done | bytes 262176 | tf_op jit(solution)/shard_map/ppermute | solution.py:256
  27.2 2.3 %collective-permute-start.5 = (f32[64,1024]{1,0:T(8,128)S(1)}, f32[64,1024]{1,0:T(8,128)S(1)}, u32[]{:S(2)}, u32[]{:S(2)}) collective-permute-start(f32[64,1024]{1,0:T(8,128)S(1)} %get-tuple-element.35), channel_id=1, source_target_pairs={{3,0},{2,1},{1,2},{0,3},{7,4},{6,5},{5,6},{4,7},{11,8},{10,9},{9,1... | collective-permute-start | bytes 786440 | tf_op jit(solution)/shard_map/ppermute | solution.py:262
  29.6 0.0 collective-permute-done.9.refs_10_
  29.6 3.3 %collective-permute-start.11 = (bf16[2,512,128]{2,1,0:T(8,128)(2,1)S(1)}, bf16[2,512,128]{2,1,0:T(8,128)(2,1)S(1)}, u32[]{:S(2)}, u32[]{:S(2)}) collective-permute-start(bf16[2,512,128]{2,1,0:T(8,128)(2,1)S(1)} %get-tuple-element.43), channel_id=1, source_target_pairs={{0,24},{4,28},{8,16},{12,20},{16,8},{20,12},{24,0},{28,4},{1,25},{... | collective-permute-start | bytes 786440 | tf_op jit(solution)/shard_map/ppermute | solution.py:256
  32.9 0.0 collective-permute-done.6.refs_7_
  32.9 0.1 collective-permute-start.10
  33.6 2.0 %collective-permute-done.5.refs_5_ = f32[64,1024]{1,0:T(8,128)S(1)} collective-permute-done((f32[64,1024]{1,0:T(8,128)S(1)}, f32[64,1024]{1,0:T(8,128)S(1)}, u32[]{:S(2)}, u32[]{:S(2)}) %collective-permute-start.5) | collective-permute-done | bytes 262176 | tf_op jit(solution)/shard_map/ppermute | solution.py:262
  35.6 3.9 %attend.3 = (f32[1,512]{1,0:T(1,128)S(1)}, f32[1,512]{1,0:T(1,128)S(1)}, f32[128,512]{1,0:T(8,128)S(1)}, bf16[512,128]{1,0:T(8,128)(2,1)S(1)}) custom-call(s32[1]{0:T(128)S(6)} %copy.7.refs_0_, s32[1,64]{1,0:T(1,128)S(1)} %copy-done.4, f32[64,1024]{1,0:T(8,128)S(1)} %get-tuple-element.32.refs_2_, f32[64,1024]{1,0:T(8,128)S(1)} %collective-permute-done.3.refs_3_, ...), custom_call_target="tpu_custom_call" | custom-call | flops 671088640 | bytes 1310720 | tf_op jit(solution)/shard_map/attend/pallas_call | solution.py:229
  39.5 0.0 collective-permute-done.11.refs_3_
  39.6 21.0 %collective-permute-done.12.refs_4_ = bf16[2,512,128]{2,1,0:T(8,128)(2,1)S(1)} collective-permute-done((bf16[2,512,128]{2,1,0:T(8,128)(2,1)S(1)}, bf16[2,512,128]{2,1,0:T(8,128)(2,1)S(1)}, u32[]{:S(2)}, u32[]{:S(2)}) %collective-permute-start.12) | collective-permute-done | bytes 262176 | tf_op jit(solution)/shard_map/ppermute | solution.py:256
  60.6 1.7 %attend.4 = (f32[1,512]{1,0:T(1,128)S(1)}, f32[1,512]{1,0:T(1,128)S(1)}, f32[128,512]{1,0:T(8,128)S(1)}) custom-call(s32[1]{0:T(128)S(6)} %copy.7.refs_0_, s32[1,64]{1,0:T(1,128)S(1)} %copy-done.4, bf16[512,128]{1,0:T(8,128)(2,1)S(1)} %get-tuple-element.41.refs_2_, bf16[2,512,128]{2,1,0:T(8,128)(2,1)S(1)} %collective-permute-done.11.refs_3_, ...), custom_call_target="tpu_custom_call" | custom-call | flops 268435456 | bytes 524288 | tf_op jit(solution)/shard_map/attend/pallas_call | solution.py:229
  62.3 1.8 %attend.5 = bf16[64,1024]{1,0:T(8,128)(2,1)} custom-call(s32[1]{0:T(128)S(6)} %copy.7.refs_0_, s32[1,64]{1,0:T(1,128)S(1)} %copy-done.4, bf16[512,128]{1,0:T(8,128)(2,1)S(1)} %get-tuple-element.41.refs_2_, bf16[2,512,128]{2,1,0:T(8,128)(2,1)S(1)} %collective-permute-done.10.refs_3_, f32[1,512]{1,0:T(1,128)S(1)} %get-tuple-element.48.refs_4_, ...), custom_call_target="tpu_custom_call" | custom-call | flops 134217728 | bytes 262144 | tf_op jit(solution)/shard_map/attend/pallas_call | solution.py:229
  (11 shorter events, 0.0 us)
Async XLA Ops:
  0.0 17.9 %copy-start = (bf16[2048,1024]{1,0:T(8,128)(2,1)S(1)}, bf16[2048,1024]{1,0:T(8,128)(2,1)}, u32[]{:S(2)}) copy-start(bf16[2048,1024]{1,0:T(8,128)(2,1)} %refs_4_.1) | copy-start | bytes 12582916
  0.0 1.4 %copy-start.3 = (bf16[1,64,8192]{2,1,0:T(8,128)(2,1)S(1)}, bf16[1,64,8192]{2,1,0:T(8,128)(2,1)}, u32[]{:S(2)}) copy-start(bf16[1,64,8192]{2,1,0:T(8,128)(2,1)} %param.6) | copy-start | bytes 3145732
  1.5 9.6 %collective-permute-start = (bf16[64,2048]{1,0:T(8,128)(2,1)S(1)}, bf16[64,2048]{1,0:T(8,128)(2,1)S(1)}, u32[]{:S(2)}, u32[]{:S(2)}) collective-permute-start(bf16[64,2048]{1,0:T(8,128)(2,1)S(1)} %get-tuple-element.29), channel_id=1, source_target_pairs={{0,1},{1,0},{2,3},{3,2},{4,5},{5,4},{6,7},{7,6},{8,9},{9,8},{10,11... | collective-permute-start | bytes 786440 | tf_op jit(solution)/shard_map/ppermute | solution.py:258
  3.6 10.3 %collective-permute-start.1 = (bf16[64,2048]{1,0:T(8,128)(2,1)S(1)}, bf16[64,2048]{1,0:T(8,128)(2,1)S(1)}, u32[]{:S(2)}, u32[]{:S(2)}) collective-permute-start(bf16[64,2048]{1,0:T(8,128)(2,1)S(1)} %get-tuple-element.30), channel_id=1, source_target_pairs={{0,2},{1,3},{2,0},{3,1},{4,6},{5,7},{6,4},{7,5},{8,10},{9,11},{10,... | collective-permute-start | bytes 786440 | tf_op jit(solution)/shard_map/ppermute | solution.py:258
  4.8 13.1 %collective-permute-start.2 = (bf16[64,2048]{1,0:T(8,128)(2,1)S(1)}, bf16[64,2048]{1,0:T(8,128)(2,1)S(1)}, u32[]{:S(2)}, u32[]{:S(2)}) collective-permute-start(bf16[64,2048]{1,0:T(8,128)(2,1)S(1)} %get-tuple-element.31), channel_id=1, source_target_pairs={{0,3},{1,2},{2,1},{3,0},{4,7},{5,6},{6,5},{7,4},{8,11},{9,10},{10,... | collective-permute-start | bytes 786440 | tf_op jit(solution)/shard_map/ppermute | solution.py:258
  4.9 1.2 %copy-start.1 = (bf16[1,512,1024]{2,1,0:T(8,128)(2,1)S(1)}, bf16[1,512,1024]{2,1,0:T(8,128)(2,1)}, u32[]{:S(2)}) copy-start(bf16[1,512,1024]{2,1,0:T(8,128)(2,1)} %param.8) | copy-start | bytes 3145732
  6.1 1.2 %copy-start.2 = (bf16[1,512,1024]{2,1,0:T(8,128)(2,1)S(1)}, bf16[1,512,1024]{2,1,0:T(8,128)(2,1)}, u32[]{:S(2)}) copy-start(bf16[1,512,1024]{2,1,0:T(8,128)(2,1)} %param.9) | copy-start | bytes 3145732
  7.6 28.0 %copy-start.4 = (s32[1,64]{1,0:T(1,128)S(1)}, s32[1,64]{1,0:T(1,128)}, u32[]{:S(2)}) copy-start(s32[1,64]{1,0:T(1,128)} %refs_1_.5) | copy-start | bytes 772
  7.6 12.9 %collective-permute-start.7 = (bf16[2,512,128]{2,1,0:T(8,128)(2,1)S(1)}, bf16[2,512,128]{2,1,0:T(8,128)(2,1)S(1)}, u32[]{:S(2)}, u32[]{:S(2)}) collective-permute-start(bf16[2,512,128]{2,1,0:T(8,128)(2,1)S(1)} %get-tuple-element.38), channel_id=1, source_target_pairs={{0,8},{4,12},{8,0},{12,4},{16,24},{20,28},{24,16},{28,20},{1,9},{5... | collective-permute-start | bytes 786440 | tf_op jit(solution)/shard_map/ppermute | solution.py:256
  9.1 18.1 %collective-permute-start.8 = (bf16[2,512,128]{2,1,0:T(8,128)(2,1)S(1)}, bf16[2,512,128]{2,1,0:T(8,128)(2,1)S(1)}, u32[]{:S(2)}, u32[]{:S(2)}) collective-permute-start(bf16[2,512,128]{2,1,0:T(8,128)(2,1)S(1)} %get-tuple-element.39), channel_id=1, source_target_pairs={{0,12},{4,8},{8,4},{12,0},{16,28},{20,24},{24,20},{28,16},{1,13},{... | collective-permute-start | bytes 786440 | tf_op jit(solution)/shard_map/ppermute | solution.py:256
  11.1 18.5 %collective-permute-start.9 = (bf16[2,512,128]{2,1,0:T(8,128)(2,1)S(1)}, bf16[2,512,128]{2,1,0:T(8,128)(2,1)S(1)}, u32[]{:S(2)}, u32[]{:S(2)}) collective-permute-start(bf16[2,512,128]{2,1,0:T(8,128)(2,1)S(1)} %get-tuple-element.40), channel_id=1, source_target_pairs={{0,16},{4,20},{8,24},{12,28},{16,0},{20,4},{24,8},{28,12},{1,17},{... | collective-permute-start | bytes 786440 | tf_op jit(solution)/shard_map/ppermute | solution.py:256
  13.9 19.1 %collective-permute-start.6 = (bf16[2,512,128]{2,1,0:T(8,128)(2,1)S(1)}, bf16[2,512,128]{2,1,0:T(8,128)(2,1)S(1)}, u32[]{:S(2)}, u32[]{:S(2)}) collective-permute-start(bf16[2,512,128]{2,1,0:T(8,128)(2,1)S(1)} %get-tuple-element.37), channel_id=1, source_target_pairs={{0,4},{4,0},{8,12},{12,8},{16,20},{20,16},{24,28},{28,24},{1,5},{5... | collective-permute-start | bytes 786440 | tf_op jit(solution)/shard_map/ppermute | solution.py:256
  20.5 12.4 %collective-permute-start.3 = (f32[64,1024]{1,0:T(8,128)S(1)}, f32[64,1024]{1,0:T(8,128)S(1)}, u32[]{:S(2)}, u32[]{:S(2)}) collective-permute-start(f32[64,1024]{1,0:T(8,128)S(1)} %get-tuple-element.33), channel_id=1, source_target_pairs={{1,0},{0,1},{3,2},{2,3},{5,4},{4,5},{7,6},{6,7},{9,8},{8,9},{11,10... | collective-permute-start | bytes 786440 | tf_op jit(solution)/shard_map/ppermute | solution.py:262
  20.6 13.1 %collective-permute-start.4 = (f32[64,1024]{1,0:T(8,128)S(1)}, f32[64,1024]{1,0:T(8,128)S(1)}, u32[]{:S(2)}, u32[]{:S(2)}) collective-permute-start(f32[64,1024]{1,0:T(8,128)S(1)} %get-tuple-element.34), channel_id=1, source_target_pairs={{2,0},{3,1},{0,2},{1,3},{6,4},{7,5},{4,6},{5,7},{10,8},{11,9},{8,1... | collective-permute-start | bytes 786440 | tf_op jit(solution)/shard_map/ppermute | solution.py:262
  27.2 8.4 %collective-permute-start.5 = (f32[64,1024]{1,0:T(8,128)S(1)}, f32[64,1024]{1,0:T(8,128)S(1)}, u32[]{:S(2)}, u32[]{:S(2)}) collective-permute-start(f32[64,1024]{1,0:T(8,128)S(1)} %get-tuple-element.35), channel_id=1, source_target_pairs={{3,0},{2,1},{1,2},{0,3},{7,4},{6,5},{5,6},{4,7},{11,8},{10,9},{9,1... | collective-permute-start | bytes 786440 | tf_op jit(solution)/shard_map/ppermute | solution.py:262
  29.6 10.0 %collective-permute-start.11 = (bf16[2,512,128]{2,1,0:T(8,128)(2,1)S(1)}, bf16[2,512,128]{2,1,0:T(8,128)(2,1)S(1)}, u32[]{:S(2)}, u32[]{:S(2)}) collective-permute-start(bf16[2,512,128]{2,1,0:T(8,128)(2,1)S(1)} %get-tuple-element.43), channel_id=1, source_target_pairs={{0,24},{4,28},{8,16},{12,20},{16,8},{20,12},{24,0},{28,4},{1,25},{... | collective-permute-start | bytes 786440 | tf_op jit(solution)/shard_map/ppermute | solution.py:256
  32.9 27.7 %collective-permute-start.12 = (bf16[2,512,128]{2,1,0:T(8,128)(2,1)S(1)}, bf16[2,512,128]{2,1,0:T(8,128)(2,1)S(1)}, u32[]{:S(2)}, u32[]{:S(2)}) collective-permute-start(bf16[2,512,128]{2,1,0:T(8,128)(2,1)S(1)} %get-tuple-element.44), channel_id=1, source_target_pairs={{0,20},{4,16},{8,28},{12,24},{16,4},{20,0},{24,12},{28,8},{1,21},{... | collective-permute-start | bytes 786440 | tf_op jit(solution)/shard_map/ppermute | solution.py:256
  32.9 29.4 %collective-permute-start.10 = (bf16[2,512,128]{2,1,0:T(8,128)(2,1)S(1)}, bf16[2,512,128]{2,1,0:T(8,128)(2,1)S(1)}, u32[]{:S(2)}, u32[]{:S(2)}) collective-permute-start(bf16[2,512,128]{2,1,0:T(8,128)(2,1)S(1)} %get-tuple-element.42), channel_id=1, source_target_pairs={{0,28},{4,24},{8,20},{12,16},{16,12},{20,8},{24,4},{28,0},{1,29},{... | collective-permute-start | bytes 786440 | tf_op jit(solution)/shard_map/ppermute | solution.py:256
where the time goes:
time: 64.4 us; the launch traced here: 64.2 us
  waiting for transfers between devices  28.3 us (44%)
  starting transfers between devices  20.5 us (32%)
  Pallas kernels  10.8 us (17%)
  local copies, waits for them, and re-layouts  3.83 us (6%)
  between operations  0.77 us (1%)
    ppermute x7, waiting for transfers between devices, own_heads(): moved[step] = lax.ppermute(block, 'seq', peers(seq_count, step))  26.3 us
    ppermute x7, starting transfers between devices, own_heads(): moved[step] = lax.ppermute(block, 'seq', peers(seq_count, step))  13.2 us
    pallas_call x3, Pallas kernels, attend(): pl.pallas_call(kernel, out_shape=out_shape, in_specs=[SMEM, VMEM] + [ANY]...  7.44 us
    ppermute x3, starting transfers between devices, own_heads(): lax.ppermute(partials[step], 'batch', [(b, a) for a, b in peers(batch_cou...  3.87 us
    unnamed x10, local copies, waits for them, and re-layouts  3.83 us
    ppermute x3, starting transfers between devices, own_heads(): blocks[step] = lax.ppermute(blocks[step], 'batch', peers(batch_count, step))  3.35 us
    pallas_call x1, Pallas kernels, project(): pl.pallas_call(kernel, grid=(columns // tile,), out_shape=[jax.ShapeDtype...  2.52 us
    ppermute x3, waiting for transfers between devices, own_heads(): lax.ppermute(partials[step], 'batch', [(b, a) for a, b in peers(batch_cou...  2 us
  transfers between devices with their start and end apart: 13, of which 3 were waited for; matrix products, arithmetic and copies ran while one was open for 0% of the time, Pallas kernels for 14%

commit v1 on v0

--- a/solution.py
+++ b/solution.py
@@ -17,6 +17,7 @@
 HBM = pl.BlockSpec(memory_space=pltpu.HBM)
 VMEM = pl.BlockSpec(memory_space=pltpu.VMEM)
 SMEM = pl.BlockSpec(memory_space=pltpu.SMEM)
+PARTNERS = 0
 SMALL = pltpu.CompilerParams(vmem_limit_bytes=24 << 20)
 LOG2E = 1.4426950408889634
 NONE_VISIBLE = -1e30
@@ -137,34 +138,74 @@
     )(*blocks, weight)
 
 
-def attend(query, chunks, steps, state, positions, lengths, seq_count, last):
+def swapped(me, pairs):
+    other = me
+    for one, two in pairs:
+        other = jnp.where(me == one, two, jnp.where(me == two, one, other))
+    return other
+
+
+def round_query(partials):
+    tokens, width = partials[0].shape
+    group = width // HD
+
+    def kernel(*refs):
+        ins, out, held, sem = refs[: len(partials)], refs[len(partials)], refs[len(partials) + 1 : -1], refs[-1]
+        copies = [pltpu.make_async_copy(src, dst, sem.at[n]) for n, (src, dst) in enumerate(zip(ins, held))]
+        for copy in copies:
+            copy.start()
+        for copy in copies:
+            copy.wait()
+        for h in range(group):
+            head = slice(h * HD, (h + 1) * HD)
+            total = held[0][:, head]
+            for ref in held[1:]:
+                total = total + ref[:, head]
+            out[h * tokens : (h + 1) * tokens, :] = total.astype(jnp.bfloat16)
+
+    return pl.pallas_call(
+        kernel,
+        out_shape=jax.ShapeDtypeStruct((group * tokens, HD), jnp.bfloat16),
+        in_specs=[ANY] * len(partials),
+        out_specs=VMEM,
+        scratch_shapes=[pltpu.VMEM(x.shape, x.dtype) for x in partials]
+        + [pltpu.SemaphoreType.DMA((len(partials),))],
+        cost_estimate=pl.CostEstimate(
+            flops=len(partials) * tokens * width,
+            transcendentals=0,
+            bytes_accessed=4 * len(partials) * tokens * width,
+        ),
+        compiler_params=SMALL,
+        name="round_query",
+    )(*partials)
+
+
+def merge(top, denom, numer, other_top, other_denom, other_numer):
+    new_top = jnp.maximum(top, other_top)
+    keep = jnp.exp2((top - new_top) * (HD**-0.5 * LOG2E))
+    weight = jnp.exp2((other_top - new_top) * (HD**-0.5 * LOG2E))
+    return new_top, denom * keep + other_denom * weight, numer * keep + other_numer * weight
+
+
+def read_state(ref):
+    return ref[HD : HD + 1, :], ref[HD + 8 : HD + 9, :], ref[:HD, :]
+
+
+def attend(queries, chunks, steps, state, positions, lengths, seq_count, pairs):
     first = state is None
     tokens = positions.shape[1]
-    group = H // KVH
-    columns = group * tokens
-    n_query = len(query)
+    columns = queries[0].shape[0]
+    n_query = len(queries)
     n_chunks = len(chunks)
     keys_here = chunks[0].shape[-2]
-    moved = [*query, *chunks]
-    inputs = [lengths, positions, *moved] + ([] if first else list(state))
-    state_shape = [
-        jax.ShapeDtypeStruct((1, columns), jnp.float32),
-        jax.ShapeDtypeStruct((1, columns), jnp.float32),
-        jax.ShapeDtypeStruct((HD, columns), jnp.float32),
-    ]
-    if last:
-        out_shape = [jax.ShapeDtypeStruct((tokens, group * HD), jnp.bfloat16)]
-    else:
-        out_shape = state_shape
-        if first:
-            out_shape = out_shape + [jax.ShapeDtypeStruct((columns, HD), jnp.bfloat16)]
+    moved = [*queries, *chunks]
+    inputs = [lengths, positions, *moved] + ([] if first else [state])
 
     def kernel(*refs):
         lengths_ref, positions_ref = refs[:2]
         moved_refs = refs[2 : 2 + len(moved)]
-        state_refs = refs[2 + len(moved) : len(inputs)]
-        outs = refs[len(inputs) : len(inputs) + len(out_shape)]
-        held = refs[len(inputs) + len(out_shape) : -1]
+        out = refs[len(inputs)]
+        held = refs[len(inputs) + 1 : -1]
         sem = refs[-1]
         copies = [
             pltpu.make_async_copy(src, dst, sem.at[n]) for n, (src, dst) in enumerate(zip(moved_refs, held))
@@ -172,25 +213,18 @@
         for copy in copies:
             copy.start()
         me = lax.axis_index("seq")
+        other = swapped(me, pairs)
         limit = jnp.minimum(positions_ref[...], lengths_ref[0] - 1)
-        limit = jnp.concatenate([limit] * group, axis=1)
+        limit = jnp.concatenate([limit] * (columns // tokens), axis=1)
         rows = lax.broadcasted_iota(jnp.int32, (keys_here, columns), 0)
         for copy in copies[:n_query]:
             copy.wait()
-        if first:
-            total = held[0][...]
-            for ref in held[1:n_query]:
-                total = total + ref[...]
-            rounded = total.astype(jnp.bfloat16)
-            q = jnp.concatenate([rounded[:, h * HD : (h + 1) * HD] for h in range(group)], axis=0)
-            if not last:
-                outs[3][...] = q
-            top = denom = numer = None
-        else:
-            q = held[0][...]
-            top, denom, numer = (ref[...] for ref in state_refs)
+        q = held[0][...]
+        if n_query == 2:
+            q = jnp.where(other == me, q, held[1][...])
+        sums = None if first else read_state(refs[len(inputs) - 1])
         for n, step in enumerate(steps):
-            start = source(me, seq_count, step) * keys_here
+            start = source(other, seq_count, step) * keys_here
             copies[n_query + n].wait()
             ref = held[n_query + n]
             score = lax.dot_general(
@@ -207,30 +241,18 @@
                 preferred_element_type=jnp.float32,
             )
             block_sum = block_sum.astype(jnp.bfloat16).astype(jnp.float32)
-            if top is None:
-                top, denom, numer = block_max, block_total, block_sum
-                continue
-            new_top = jnp.maximum(top, block_max)
-            keep = jnp.exp2((top - new_top) * (HD**-0.5 * LOG2E))
-            weight = jnp.exp2((block_max - new_top) * (HD**-0.5 * LOG2E))
-            denom = denom * keep + block_total * weight
-            numer = numer * keep + block_sum * weight
-            top = new_top
-        if last:
-            result = numer / denom
-            for h in range(group):
-                part = result[:, h * tokens : (h + 1) * tokens]
-                outs[0][:, h * HD : (h + 1) * HD] = jnp.transpose(part).astype(jnp.bfloat16)
-        else:
-            outs[0][...] = top
-            outs[1][...] = denom
-            outs[2][...] = numer
-
-    return pl.pallas_call(
-        kernel,
-        out_shape=out_shape,
+            block = block_max, block_total, block_sum
+            sums = block if sums is None else merge(*sums, *block)
+        top, denom, numer = sums
+        out[:HD, :] = numer
+        out[HD : HD + 8, :] = jnp.broadcast_to(top, (8, columns))
+        out[HD + 8 :, :] = jnp.broadcast_to(denom, (8, columns))
+
+    return pl.pallas_call(
+        kernel,
+        out_shape=jax.ShapeDtypeStruct((HD + 16, columns), jnp.float32),
         in_specs=[SMEM, VMEM] + [ANY] * len(moved) + [VMEM] * (len(inputs) - 2 - len(moved)),
-        out_specs=[VMEM] * len(out_shape),
+        out_specs=VMEM,
         scratch_shapes=[pltpu.VMEM(x.shape, x.dtype) for x in moved]
         + [pltpu.SemaphoreType.DMA((len(moved),))],
         cost_estimate=pl.CostEstimate(
@@ -243,30 +265,81 @@
     )(*inputs)
 
 
+def finish(near, far, received, tokens, pairs):
+    columns = near.shape[1]
+    group = columns // tokens
+
+    def kernel(near_ref, far_ref, received_ref, out):
+        me = lax.axis_index("seq")
+        mine = swapped(me, pairs) == me
+        far_sums = [
+            jnp.where(mine, one, two) for one, two in zip(read_state(far_ref), read_state(received_ref))
+        ]
+        _, denom, numer = merge(*read_state(near_ref), *far_sums)
+        result = numer / denom
+        for h in range(group):
+            part = result[:, h * tokens : (h + 1) * tokens]
+            out[:, h * HD : (h + 1) * HD] = jnp.transpose(part).astype(jnp.bfloat16)
+
+    return pl.pallas_call(
+        kernel,
+        out_shape=jax.ShapeDtypeStruct((tokens, group * HD), jnp.bfloat16),
+        in_specs=[VMEM] * 3,
+        out_specs=VMEM,
+        cost_estimate=pl.CostEstimate(
+            flops=8 * HD * columns, transcendentals=0, bytes_accessed=12 * HD * columns
+        ),
+        compiler_params=SMALL,
+        name="finish",
+    )(near, far, received)
+
+
+def partner_pairs(count):
+    half = count // 2
+    across = half + half // 2
+    return [(one, one ^ across) for one in range(half // 2, half)][:PARTNERS]
+
+
 def own_heads(inputs, w_query, cache_keys, cache_values, lengths, positions):
     seq_count = lax.axis_size("seq")
     batch_count = lax.axis_size("batch")
+    half = seq_count // 2
     order = seq_order(seq_count)
-    key_rows, value_rows, tokens = cache_keys[0], cache_values[0], inputs[0]
-    packed = pack_cache(key_rows, value_rows, seq_count, order[:3])
+    pairs = partner_pairs(seq_count)
+    meet = [*pairs, *((two, one) for one, two in pairs)]
+    swap = dict(meet)
+    key_rows, value_rows, tokens = (
+        pltpu.with_memory_space_constraint(x[0], pltpu.HBM) for x in (cache_keys, cache_values, inputs)
+    )
     blocks = list(pack_features(tokens, batch_count))
-    packed = [*packed, *pack_cache(key_rows, value_rows, seq_count, [*order[3:], 0])]
+    packed = pack_cache(key_rows, value_rows, seq_count, order[:1])
+    packed = [*packed, *pack_cache(key_rows, value_rows, seq_count, [*order[1:], 0])]
     moved = {0: packed[-1]}
     for step, block in zip(order, packed):
-        moved[step] = lax.ppermute(block, "seq", peers(seq_count, step))
+        to = peers(seq_count, step)
+        if step >= half:
+            to = [(a, swap.get(b, b)) for a, b in to]
+        moved[step] = lax.ppermute(block, "seq", to)
     for step in range(1, batch_count):
         blocks[step] = lax.ppermute(blocks[step], "batch", peers(batch_count, step))
-    partials = project(blocks, w_query)
+    partials = project(blocks, pltpu.with_memory_space_constraint(w_query, pltpu.HBM))
     back = [partials[0]]
     for step in range(1, batch_count):
         back.append(lax.ppermute(partials[step], "batch", [(b, a) for a, b in peers(batch_count, step)]))
+    query = round_query(back)
+    queries = [query]
+    if pairs:
+        queries.append(lax.ppermute(query, "seq", meet))
     attend_ = functools.partial(attend, positions=positions, lengths=lengths, seq_count=seq_count)
-    half = seq_count // 2
-    early, middle, late = [*range(half), order[0]], order[half - 1 : -2], order[-2:-1]
-    *state, query = attend_(back, [moved[s] for s in early], early, None, last=False)
-    state = attend_([query], [moved[s] for s in middle], middle, state, last=False)
-    (out,) = attend_([query], [moved[s] for s in late], late, state, last=True)
-    return out[None]
+    early, middle, late = [*range(half)], [order[0], order[half - 1]], order[half:-1]
+    near = attend_([query], [moved[s] for s in early], early, None, pairs=[])
+    far = None
+    for steps in (middle, late[:1], late[1:]):
+        far = attend_(queries, [moved[s] for s in steps], steps, far, pairs=pairs)
+    received = far
+    if pairs:
+        received = lax.ppermute(far, "seq", meet)
+    return finish(near, far, received, positions.shape[1], pairs)[None]
 
 
 def split_positions(inputs, w_query, cache_keys, cache_values, lengths, positions):

time: 64.4 us -> 64.3 us (level)
  the two profiles are of different devices: /device:TPU:1 before, /device:TPU:0 now
where the time goes in v1:
time: 64.3 us; the launch traced here: 64.1 us
  starting transfers between devices  26.1 us (41%)
  waiting for transfers between devices  21.4 us (33%)
  Pallas kernels  15.8 us (25%)
  between operations  0.78 us (1%)
    ppermute x7, starting transfers between devices, own_heads(): moved[step] = lax.ppermute(block, 'seq', to)  17.9 us
    ppermute x7, waiting for transfers between devices, own_heads(): moved[step] = lax.ppermute(block, 'seq', to)  11.1 us
    pallas_call x4, Pallas kernels, attend(): pl.pallas_call(kernel, out_shape=jax.ShapeDtypeStruct((HD + 16, columns),...  6.85 us
    ppermute x3, waiting for transfers between devices, own_heads(): lax.ppermute(partials[step], 'batch', [(b, a) for a, b in peers(batch_cou...  5.7 us
    ppermute x3, waiting for transfers between devices, own_heads(): blocks[step] = lax.ppermute(blocks[step], 'batch', peers(batch_count, step))  4.61 us
    ppermute x3, starting transfers between devices, own_heads(): blocks[step] = lax.ppermute(blocks[step], 'batch', peers(batch_count, step))  4.57 us
    pallas_call x1, Pallas kernels, project(): pl.pallas_call(kernel, grid=(columns // tile,), out_shape=[jax.ShapeDtype...  4.01 us
    ppermute x3, starting transfers between devices, own_heads(): lax.ppermute(partials[step], 'batch', [(b, a) for a, b in peers(batch_cou...  3.55 us
  transfers between devices with their start and end apart: 13, of which 6 were waited for; matrix products, arithmetic and copies ran while one was open for 0% of the time, Pallas kernels for 17%

profile of v1, /device:TPU:0, one launch (start us, length us, event | category | flops | bytes accessed | tf_op | source)
XLA Modules:
  0.0 64.1 jit_solution(2217011349386502166)
XLA Ops:
  0.0 1.2 %pack_features.1 = (bf16[64,2048]{1,0:T(8,128)(2,1)S(1)}, bf16[64,2048]{1,0:T(8,128)(2,1)S(1)}, bf16[64,2048]{1,0:T(8,128)(2,1)S(1)}, bf16[64,2048]{1,0:T(8,128)(2,1)S(1)}) custom-call(bf16[64,8192]{1,0:T(8,128)(2,1)} %bitcast.8), custom_call_target="tpu_custom_call" | custom-call | bytes 2097152 | tf_op jit(solution)/shard_map/pack_features/pallas_call | solution.py:93
  1.2 3.0 %collective-permute-start = (bf16[64,2048]{1,0:T(8,128)(2,1)S(1)}, bf16[64,2048]{1,0:T(8,128)(2,1)S(1)}, u32[]{:S(2)}, u32[]{:S(2)}) collective-permute-start(bf16[64,2048]{1,0:T(8,128)(2,1)S(1)} %get-tuple-element.21), channel_id=1, source_target_pairs={{0,1},{1,0},{2,3},{3,2},{4,5},{5,4},{6,7},{7,6},{8,9},{9,8},{10,11... | collective-permute-start | bytes 786440 | tf_op jit(solution)/shard_map/ppermute | solution.py:324
  4.3 1.5 %collective-permute-start.1 = (bf16[64,2048]{1,0:T(8,128)(2,1)S(1)}, bf16[64,2048]{1,0:T(8,128)(2,1)S(1)}, u32[]{:S(2)}, u32[]{:S(2)}) collective-permute-start(bf16[64,2048]{1,0:T(8,128)(2,1)S(1)} %get-tuple-element.22), channel_id=1, source_target_pairs={{0,2},{1,3},{2,0},{3,1},{4,6},{5,7},{6,4},{7,5},{8,10},{9,11},{10,... | collective-permute-start | bytes 786440 | tf_op jit(solution)/shard_map/ppermute | solution.py:324
  5.8 0.0 collective-permute-start.2
  5.8 1.0 %pack_cache.3 = bf16[2,512,128]{2,1,0:T(8,128)(2,1)S(1)} custom-call(bf16[512,1024]{1,0:T(8,128)(2,1)} %bitcast.4, bf16[512,1024]{1,0:T(8,128)(2,1)} %bitcast.6), custom_call_target="tpu_custom_call" | custom-call | bytes 524288 | tf_op jit(solution)/shard_map/pack_cache/pallas_call | solution.py:63
  6.8 0.0 copy-start
  6.8 3.1 %collective-permute-start.11 = (bf16[2,512,128]{2,1,0:T(8,128)(2,1)S(1)}, bf16[2,512,128]{2,1,0:T(8,128)(2,1)S(1)}, u32[]{:S(2)}, u32[]{:S(2)}) collective-permute-start(bf16[2,512,128]{2,1,0:T(8,128)(2,1)S(1)} %pack_cache.3), channel_id=1, source_target_pairs={{0,16},{4,20},{8,24},{12,28},{16,0},{20,4},{24,8},{28,12},{1,17},{... | collective-permute-start | bytes 786440 | tf_op jit(solution)/shard_map/ppermute | solution.py:322
  9.9 1.7 %pack_cache.2 = (bf16[2,512,128]{2,1,0:T(8,128)(2,1)S(1)}, bf16[2,512,128]{2,1,0:T(8,128)(2,1)S(1)}, bf16[2,512,128]{2,1,0:T(8,128)(2,1)S(1)}, bf16[2,512,128]{2...) custom-call(bf16[512,1024]{1,0:T(8,128)(2,1)} %bitcast.5, ...), custom_call_target="tpu_custom_call" | custom-call | bytes 3670016 | tf_op jit(solution)/shard_map/pack_cache/pallas_call | solution.py:63
  11.6 1.4 %collective-permute-start.12 = (bf16[2,512,128]{2,1,0:T(8,128)(2,1)S(1)}, bf16[2,512,128]{2,1,0:T(8,128)(2,1)S(1)}, u32[]{:S(2)}, u32[]{:S(2)}) collective-permute-start(bf16[2,512,128]{2,1,0:T(8,128)(2,1)S(1)} %get-tuple-element.34), channel_id=1, source_target_pairs={{0,24},{4,28},{8,16},{12,20},{16,8},{20,12},{24,0},{28,4},{1,25},{... | collective-permute-start | bytes 786440 | tf_op jit(solution)/shard_map/ppermute | solution.py:322
  13.0 4.6 %collective-permute-done.1.refs_2_ = bf16[64,2048]{1,0:T(8,128)(2,1)S(1)} collective-permute-done((bf16[64,2048]{1,0:T(8,128)(2,1)S(1)}, bf16[64,2048]{1,0:T(8,128)(2,1)S(1)}, u32[]{:S(2)}, u32[]{:S(2)}) %collective-permute-start.1) | collective-permute-done | bytes 262176 | tf_op jit(solution)/shard_map/ppermute | solution.py:324
  17.6 0.0 collective-permute-done.2.refs_3_
  17.6 4.0 %project.1 = (f32[64,1024]{1,0:T(8,128)S(1)}, f32[64,1024]{1,0:T(8,128)S(1)}, f32[64,1024]{1,0:T(8,128)S(1)}, f32[64,1024]{1,0:T(8,128)S(1)}) custom-call(bf16[64,2048]{1,0:T(8,128)(2,1)S(1)} %get-tuple-element.20.refs_0_, bf16[64,2048]{1,0:T(8,128)(2,1)S(1)} %collective-permute-done.refs_1_, bf16[64,2048]{1,0:T(8,128)(2,1)S(1)} %collective-permute-done.1.refs_2_, ...), custom_call_target="tpu_custom_call" | custom-call | flops 1073741824 | bytes 7340032 | tf_op jit(solution)/shard_map/project/pallas_call | solution.py:123
  21.7 1.3 %collective-permute-start.3 = (f32[64,1024]{1,0:T(8,128)S(1)}, f32[64,1024]{1,0:T(8,128)S(1)}, u32[]{:S(2)}, u32[]{:S(2)}) collective-permute-start(f32[64,1024]{1,0:T(8,128)S(1)} %get-tuple-element.25), channel_id=1, source_target_pairs={{1,0},{0,1},{3,2},{2,3},{5,4},{4,5},{7,6},{6,7},{9,8},{8,9},{11,10... | collective-permute-start | bytes 786440 | tf_op jit(solution)/shard_map/ppermute | solution.py:328
  23.0 0.8 %collective-permute-start.4 = (f32[64,1024]{1,0:T(8,128)S(1)}, f32[64,1024]{1,0:T(8,128)S(1)}, u32[]{:S(2)}, u32[]{:S(2)}) collective-permute-start(f32[64,1024]{1,0:T(8,128)S(1)} %get-tuple-element.26), channel_id=1, source_target_pairs={{2,0},{3,1},{0,2},{1,3},{6,4},{7,5},{4,6},{5,7},{10,8},{11,9},{8,1... | collective-permute-start | bytes 786440 | tf_op jit(solution)/shard_map/ppermute | solution.py:328
  23.8 1.4 %collective-permute-start.5 = (f32[64,1024]{1,0:T(8,128)S(1)}, f32[64,1024]{1,0:T(8,128)S(1)}, u32[]{:S(2)}, u32[]{:S(2)}) collective-permute-start(f32[64,1024]{1,0:T(8,128)S(1)} %get-tuple-element.27), channel_id=1, source_target_pairs={{3,0},{2,1},{1,2},{0,3},{7,4},{6,5},{5,6},{4,7},{11,8},{10,9},{9,1... | collective-permute-start | bytes 786440 | tf_op jit(solution)/shard_map/ppermute | solution.py:328
  25.2 2.6 %collective-permute-done.11.refs_3_ = bf16[2,512,128]{2,1,0:T(8,128)(2,1)S(1)} collective-permute-done((bf16[2,512,128]{2,1,0:T(8,128)(2,1)S(1)}, bf16[2,512,128]{2,1,0:T(8,128)(2,1)S(1)}, u32[]{:S(2)}, u32[]{:S(2)}) %collective-permute-start.11) | collective-permute-done | bytes 262176 | tf_op jit(solution)/shard_map/ppermute | solution.py:322
  27.8 2.0 %collective-permute-start.9 = (bf16[2,512,128]{2,1,0:T(8,128)(2,1)S(1)}, bf16[2,512,128]{2,1,0:T(8,128)(2,1)S(1)}, u32[]{:S(2)}, u32[]{:S(2)}) collective-permute-start(bf16[2,512,128]{2,1,0:T(8,128)(2,1)S(1)} %get-tuple-element.32), channel_id=1, source_target_pairs={{0,28},{4,24},{8,20},{12,16},{16,12},{20,8},{24,4},{28,0},{1,29},{... | collective-permute-start | bytes 786440 | tf_op jit(solution)/shard_map/ppermute | solution.py:322
  29.8 1.1 %collective-permute-done.3.refs_1_ = f32[64,1024]{1,0:T(8,128)S(1)} collective-permute-done((f32[64,1024]{1,0:T(8,128)S(1)}, f32[64,1024]{1,0:T(8,128)S(1)}, u32[]{:S(2)}, u32[]{:S(2)}) %collective-permute-start.3) | collective-permute-done | bytes 262176 | tf_op jit(solution)/shard_map/ppermute | solution.py:328
  30.9 0.0 collective-permute-start.6
  30.9 4.6 %collective-permute-done.4.refs_2_ = f32[64,1024]{1,0:T(8,128)S(1)} collective-permute-done((f32[64,1024]{1,0:T(8,128)S(1)}, f32[64,1024]{1,0:T(8,128)S(1)}, u32[]{:S(2)}, u32[]{:S(2)}) %collective-permute-start.4) | collective-permute-done | bytes 262176 | tf_op jit(solution)/shard_map/ppermute | solution.py:328
  35.5 11.4 %collective-permute-start.7 = (bf16[2,512,128]{2,1,0:T(8,128)(2,1)S(1)}, bf16[2,512,128]{2,1,0:T(8,128)(2,1)S(1)}, u32[]{:S(2)}, u32[]{:S(2)}) collective-permute-start(bf16[2,512,128]{2,1,0:T(8,128)(2,1)S(1)} %get-tuple-element.30), channel_id=1, source_target_pairs={{0,8},{4,12},{8,0},{12,4},{16,24},{20,28},{24,16},{28,20},{1,9},{5... | collective-permute-start | bytes 786440 | tf_op jit(solution)/shard_map/ppermute | solution.py:322
  46.9 0.0 collective-permute-done.5.refs_3_
  47.6 0.2 round_query.1.refs_2_
  47.7 1.7 %attend.5.refs_4_ = f32[144,512]{1,0:T(8,128)S(1)} custom-call(s32[1]{0:T(128)S(6)} %copy.7.refs_0_, s32[1,64]{1,0:T(1,128)S(1)} %copy-done, bf16[512,128]{1,0:T(8,128)(2,1)S(1)} %round_query.1.refs_2_, bf16[2,512,128]{2,1,0:T(8,128)(2,1)S(1)} %collective-permute-done.11.refs_3_, bf16[2,512,128]{2,1,0:T(8,128)(2,1)S(1)} %collective-permute-done.12.refs_4_), custom_call_target="tpu_custom_call" | custom-call | flops 268435456 | bytes 524288 | tf_op jit(solution)/shard_map/attend/pallas_call | solution.py:251
  49.5 0.0 collective-permute-done.10.refs_3_
  49.5 1.0 %attend.6.refs_4_ = f32[144,512]{1,0:T(8,128)S(1)} custom-call(s32[1]{0:T(128)S(6)} %copy.7.refs_0_, s32[1,64]{1,0:T(1,128)S(1)} %copy-done, bf16[512,128]{1,0:T(8,128)(2,1)S(1)} %round_query.1.refs_2_, bf16[2,512,128]{2,1,0:T(8,128)(2,1)S(1)} %collective-permute-done.10.refs_3_, f32[144,512]{1,0:T(8,128)S(1)} %attend.5.refs_4_), custom_call_target="tpu_custom_call" | custom-call | flops 134217728 | bytes 262144 | tf_op jit(solution)/shard_map/attend/pallas_call | solution.py:251
  50.5 1.0 %attend.7.far_ref.received_ref = f32[144,512]{1,0:T(8,128)S(1)} custom-call(s32[1]{0:T(128)S(6)} %copy.7.refs_0_, s32[1,64]{1,0:T(1,128)S(1)} %copy-done, bf16[512,128]{1,0:T(8,128)(2,1)S(1)} %round_query.1.refs_2_, bf16[2,512,128]{2,1,0:T(8,128)(2,1)S(1)} %collective-permute-done.9.refs_3_, f32[144,512]{1,0:T(8,128)S(1)} %attend.6.refs_4_), custom_call_target="tpu_custom_call" | custom-call | flops 134217728 | bytes 262144 | tf_op jit(solution)/shard_map/attend/pallas_call | solution.py:251
  51.5 0.0 collective-permute-done.6.refs_4_
  51.5 3.4 %collective-permute-done.7.refs_5_ = bf16[2,512,128]{2,1,0:T(8,128)(2,1)S(1)} collective-permute-done((bf16[2,512,128]{2,1,0:T(8,128)(2,1)S(1)}, bf16[2,512,128]{2,1,0:T(8,128)(2,1)S(1)}, u32[]{:S(2)}, u32[]{:S(2)}) %collective-permute-start.7) | collective-permute-done | bytes 262176 | tf_op jit(solution)/shard_map/ppermute | solution.py:322
  54.9 5.2 %collective-permute-done.8.refs_6_ = bf16[2,512,128]{2,1,0:T(8,128)(2,1)S(1)} collective-permute-done((bf16[2,512,128]{2,1,0:T(8,128)(2,1)S(1)}, bf16[2,512,128]{2,1,0:T(8,128)(2,1)S(1)}, u32[]{:S(2)}, u32[]{:S(2)}) %collective-permute-start.8) | collective-permute-done | bytes 262176 | tf_op jit(solution)/shard_map/ppermute | solution.py:322
  60.1 3.1 %attend.4.near_ref = f32[144,512]{1,0:T(8,128)S(1)} custom-call(s32[1]{0:T(128)S(6)} %copy.7.refs_0_, s32[1,64]{1,0:T(1,128)S(1)} %copy-done, bf16[512,128]{1,0:T(8,128)(2,1)S(1)} %round_query.1.refs_2_, bf16[2,512,128]{2,1,0:T(8,128)(2,1)S(1)} %get-tuple-element.28.refs_3_, bf16[2,512,128]{2,1,0:T(8,128)(2,1)S(1)} %collective-permute-done.6.refs_4_, ...), custom_call_target="tpu_custom_call" | custom-call | flops 536870912 | bytes 1048576 | tf_op jit(solution)/shard_map/attend/pallas_call | solution.py:251
  63.2 0.9 %finish.1 = bf16[64,1024]{1,0:T(8,128)(2,1)} custom-call(f32[144,512]{1,0:T(8,128)S(1)} %attend.4.near_ref, f32[144,512]{1,0:T(8,128)S(1)} %attend.7.far_ref.received_ref, f32[144,512]{1,0:T(8,128)S(1)} %attend.7.far_ref.received_ref), custom_call_target="tpu_custom_call" | custom-call | flops 524288 | bytes 786432 | tf_op jit(solution)/shard_map/finish/pallas_call | solution.py:284
  (6 shorter events, 0.0 us)
Async XLA Ops:
  1.2 11.8 %collective-permute-start = (bf16[64,2048]{1,0:T(8,128)(2,1)S(1)}, bf16[64,2048]{1,0:T(8,128)(2,1)S(1)}, u32[]{:S(2)}, u32[]{:S(2)}) collective-permute-start(bf16[64,2048]{1,0:T(8,128)(2,1)S(1)} %get-tuple-element.21), channel_id=1, source_target_pairs={{0,1},{1,0},{2,3},{3,2},{4,5},{5,4},{6,7},{7,6},{8,9},{9,8},{10,11... | collective-permute-start | bytes 786440 | tf_op jit(solution)/shard_map/ppermute | solution.py:324
  4.3 13.4 %collective-permute-start.1 = (bf16[64,2048]{1,0:T(8,128)(2,1)S(1)}, bf16[64,2048]{1,0:T(8,128)(2,1)S(1)}, u32[]{:S(2)}, u32[]{:S(2)}) collective-permute-start(bf16[64,2048]{1,0:T(8,128)(2,1)S(1)} %get-tuple-element.22), channel_id=1, source_target_pairs={{0,2},{1,3},{2,0},{3,1},{4,6},{5,7},{6,4},{7,5},{8,10},{9,11},{10,... | collective-permute-start | bytes 786440 | tf_op jit(solution)/shard_map/ppermute | solution.py:324
  5.8 11.9 %collective-permute-start.2 = (bf16[64,2048]{1,0:T(8,128)(2,1)S(1)}, bf16[64,2048]{1,0:T(8,128)(2,1)S(1)}, u32[]{:S(2)}, u32[]{:S(2)}) collective-permute-start(bf16[64,2048]{1,0:T(8,128)(2,1)S(1)} %get-tuple-element.23), channel_id=1, source_target_pairs={{0,3},{1,2},{2,1},{3,0},{4,7},{5,6},{6,5},{7,4},{8,11},{9,10},{10,... | collective-permute-start | bytes 786440 | tf_op jit(solution)/shard_map/ppermute | solution.py:324
  6.8 40.9 %copy-start = (s32[1,64]{1,0:T(1,128)S(1)}, s32[1,64]{1,0:T(1,128)}, u32[]{:S(2)}) copy-start(s32[1,64]{1,0:T(1,128)} %refs_1_.7) | copy-start | bytes 772
  6.8 21.0 %collective-permute-start.11 = (bf16[2,512,128]{2,1,0:T(8,128)(2,1)S(1)}, bf16[2,512,128]{2,1,0:T(8,128)(2,1)S(1)}, u32[]{:S(2)}, u32[]{:S(2)}) collective-permute-start(bf16[2,512,128]{2,1,0:T(8,128)(2,1)S(1)} %pack_cache.3), channel_id=1, source_target_pairs={{0,16},{4,20},{8,24},{12,28},{16,0},{20,4},{24,8},{28,12},{1,17},{... | collective-permute-start | bytes 786440 | tf_op jit(solution)/shard_map/ppermute | solution.py:322
  11.6 16.2 %collective-permute-start.12 = (bf16[2,512,128]{2,1,0:T(8,128)(2,1)S(1)}, bf16[2,512,128]{2,1,0:T(8,128)(2,1)S(1)}, u32[]{:S(2)}, u32[]{:S(2)}) collective-permute-start(bf16[2,512,128]{2,1,0:T(8,128)(2,1)S(1)} %get-tuple-element.34), channel_id=1, source_target_pairs={{0,24},{4,28},{8,16},{12,20},{16,8},{20,12},{24,0},{28,4},{1,25},{... | collective-permute-start | bytes 786440 | tf_op jit(solution)/shard_map/ppermute | solution.py:322
  21.7 9.2 %collective-permute-start.3 = (f32[64,1024]{1,0:T(8,128)S(1)}, f32[64,1024]{1,0:T(8,128)S(1)}, u32[]{:S(2)}, u32[]{:S(2)}) collective-permute-start(f32[64,1024]{1,0:T(8,128)S(1)} %get-tuple-element.25), channel_id=1, source_target_pairs={{1,0},{0,1},{3,2},{2,3},{5,4},{4,5},{7,6},{6,7},{9,8},{8,9},{11,10... | collective-permute-start | bytes 786440 | tf_op jit(solution)/shard_map/ppermute | solution.py:328
  23.0 12.5 %collective-permute-start.4 = (f32[64,1024]{1,0:T(8,128)S(1)}, f32[64,1024]{1,0:T(8,128)S(1)}, u32[]{:S(2)}, u32[]{:S(2)}) collective-permute-start(f32[64,1024]{1,0:T(8,128)S(1)} %get-tuple-element.26), channel_id=1, source_target_pairs={{2,0},{3,1},{0,2},{1,3},{6,4},{7,5},{4,6},{5,7},{10,8},{11,9},{8,1... | collective-permute-start | bytes 786440 | tf_op jit(solution)/shard_map/ppermute | solution.py:328
  23.8 23.1 %collective-permute-start.5 = (f32[64,1024]{1,0:T(8,128)S(1)}, f32[64,1024]{1,0:T(8,128)S(1)}, u32[]{:S(2)}, u32[]{:S(2)}) collective-permute-start(f32[64,1024]{1,0:T(8,128)S(1)} %get-tuple-element.27), channel_id=1, source_target_pairs={{3,0},{2,1},{1,2},{0,3},{7,4},{6,5},{5,6},{4,7},{11,8},{10,9},{9,1... | collective-permute-start | bytes 786440 | tf_op jit(solution)/shard_map/ppermute | solution.py:328
  27.8 21.7 %collective-permute-start.10 = (bf16[2,512,128]{2,1,0:T(8,128)(2,1)S(1)}, bf16[2,512,128]{2,1,0:T(8,128)(2,1)S(1)}, u32[]{:S(2)}, u32[]{:S(2)}) collective-permute-start(bf16[2,512,128]{2,1,0:T(8,128)(2,1)S(1)} %get-tuple-element.33), channel_id=1, source_target_pairs={{0,20},{4,16},{8,28},{12,24},{16,4},{20,0},{24,12},{28,8},{1,21},{... | collective-permute-start | bytes 786440 | tf_op jit(solution)/shard_map/ppermute | solution.py:322
  27.8 22.7 %collective-permute-start.9 = (bf16[2,512,128]{2,1,0:T(8,128)(2,1)S(1)}, bf16[2,512,128]{2,1,0:T(8,128)(2,1)S(1)}, u32[]{:S(2)}, u32[]{:S(2)}) collective-permute-start(bf16[2,512,128]{2,1,0:T(8,128)(2,1)S(1)} %get-tuple-element.32), channel_id=1, source_target_pairs={{0,28},{4,24},{8,20},{12,16},{16,12},{20,8},{24,4},{28,0},{1,29},{... | collective-permute-start | bytes 786440 | tf_op jit(solution)/shard_map/ppermute | solution.py:322
  30.9 20.6 %collective-permute-start.6 = (bf16[2,512,128]{2,1,0:T(8,128)(2,1)S(1)}, bf16[2,512,128]{2,1,0:T(8,128)(2,1)S(1)}, u32[]{:S(2)}, u32[]{:S(2)}) collective-permute-start(bf16[2,512,128]{2,1,0:T(8,128)(2,1)S(1)} %get-tuple-element.29), channel_id=1, source_target_pairs={{0,4},{4,0},{8,12},{12,8},{16,20},{20,16},{24,28},{28,24},{1,5},{5... | collective-permute-start | bytes 786440 | tf_op jit(solution)/shard_map/ppermute | solution.py:322
  35.5 19.4 %collective-permute-start.7 = (bf16[2,512,128]{2,1,0:T(8,128)(2,1)S(1)}, bf16[2,512,128]{2,1,0:T(8,128)(2,1)S(1)}, u32[]{:S(2)}, u32[]{:S(2)}) collective-permute-start(bf16[2,512,128]{2,1,0:T(8,128)(2,1)S(1)} %get-tuple-element.30), channel_id=1, source_target_pairs={{0,8},{4,12},{8,0},{12,4},{16,24},{20,28},{24,16},{28,20},{1,9},{5... | collective-permute-start | bytes 786440 | tf_op jit(solution)/shard_map/ppermute | solution.py:322
  46.9 13.2 %collective-permute-start.8 = (bf16[2,512,128]{2,1,0:T(8,128)(2,1)S(1)}, bf16[2,512,128]{2,1,0:T(8,128)(2,1)S(1)}, u32[]{:S(2)}, u32[]{:S(2)}) collective-permute-start(bf16[2,512,128]{2,1,0:T(8,128)(2,1)S(1)} %get-tuple-element.31), channel_id=1, source_target_pairs={{0,12},{4,8},{8,4},{12,0},{16,28},{20,24},{24,20},{28,16},{1,13},{... | collective-permute-start | bytes 786440 | tf_op jit(solution)/shard_map/ppermute | solution.py:322
